TPU v7x, 256 devices: a whole 4x4x8 slice. The times are simulated.
256 devices in a mesh: outer: 32 (over z_lo, x, core), inner: 8 (over y, z_hi).
Axes of the slice: x: 4, y: 4, z: 8 (z_hi: 2, z_lo: 4; z = z_hi * 4 + z_lo), core: 2. Of those that a mesh axis runs over, the one named last changes fastest.
Arguments:
- qkv: bfloat16 [16384, 8, 10, 128], P(('outer', 'inner')), may hold values from -96 to 96
- key_codes: int32 [4096, 8, 16], P('outer', 'inner'), may hold values from 0 to 255
- codebooks: bfloat16 [8, 256, 128], P('inner'), may hold values from -4 to 4
- value_codes: bfloat16 [4096, 8, 128], P('outer', 'inner'), may hold values from -4 to 4
- value_scales: float32 [4096, 8], P('outer', 'inner'), may hold values from 0.25 to 4
- block_ids: int32 [32], P('outer'), may hold values from 0 to 31, each once
Outputs:
- attended: bfloat16 [16384, 8, 8, 128], P(('outer', 'inner'))
All inputs are finite; a program needn't handle non-finite values.
Results may differ from a plain program's by a relative error of at most 0.011.
Values may be sent and summed in bfloat16 or wider, within the bound.
A program may use at most 64 MiB of HBM per device.

v0:
```python
import math
import jax
import jax.numpy as jnp
from jax import lax
from jax.sharding import PartitionSpec as P

rope_base = 500000.0


def rotate(tensor, position):
    half_dim = tensor.shape[-1] // 2
    ladder = jnp.arange(half_dim, dtype=jnp.float32)
    inverse = jnp.exp(ladder * jnp.float32(-2.0 * math.log(rope_base) / tensor.shape[-1]))
    angles = position.astype(jnp.float32)[:, None] * inverse[None, :]
    target = (position.shape[0],) + (1,) * (tensor.ndim - 2) + (half_dim,)
    cosine = jnp.cos(angles).reshape(target)
    sine_part = jnp.sin(angles).reshape(target)
    floats = tensor.astype(jnp.float32)
    first_half = floats[..., :half_dim]
    second_half = floats[..., half_dim:]
    return jnp.concatenate(
        [
            first_half * cosine - second_half * sine_part,
            second_half * cosine + first_half * sine_part,
        ],
        axis=-1,
    )


def decode_block(key_codes, codebooks):
    block_rows, kv_local, group_count = key_codes.shape
    entries = codebooks.shape[1]
    head_dim = codebooks.shape[2]
    ladder = lax.broadcasted_iota(jnp.int32, (1, 1, 1, entries), 3).astype(jnp.float32)
    one_hot = (key_codes.astype(jnp.float32)[..., None] == ladder).astype(jnp.bfloat16)
    code_table = codebooks.reshape(kv_local, entries, group_count, head_dim // group_count)
    decoded = jnp.einsum("bkgc,kcgd->bkgd", one_hot, code_table, preferred_element_type=jnp.float32)
    return decoded.reshape(block_rows, kv_local, head_dim)


def span_of():
    return 1024


def absorb(state, queries, key_rows, value_rows, allowed):
    running_max, running_sum, weighted = state
    scores = jnp.einsum(
        "tkgd,nkd->tkgn", queries, key_rows, preferred_element_type=jnp.float32
    ) * queries.shape[-1] ** (-0.5)
    if allowed is not None:
        scores = jnp.where(allowed[:, None, None, :], scores, -jnp.inf)
    new_max = jnp.maximum(running_max, jnp.max(scores, axis=-1))
    decay_factor = jnp.exp(running_max - new_max)
    weights = jnp.exp(scores - new_max[..., None])
    running_sum = running_sum * decay_factor + jnp.sum(weights, axis=-1)
    weighted = weighted * decay_factor[..., None] + jnp.einsum(
        "tkgn,nkd->tkgd",
        weights.astype(jnp.bfloat16),
        value_rows,
        preferred_element_type=jnp.float32,
    )
    return (new_max, running_sum, weighted)


def shards(qkv, key_codes, codebooks, value_codes, value_scales, block_ids):
    group_heads = qkv.shape[2] - 2
    head_dim = qkv.shape[3]
    block_rows = key_codes.shape[0]
    prefix_len = block_rows * lax.axis_size("outer")
    prefix_values = (value_codes.astype(jnp.float32) * value_scales[:, :, None]).astype(
        jnp.bfloat16
    )
    exchanged = lax.all_to_all(qkv, "inner", split_axis=1, concat_axis=0, tiled=True)
    stretch_rows = exchanged.shape[0]
    kv_local = exchanged.shape[1]
    local_pos = jnp.arange(stretch_rows, dtype=jnp.int32)
    stretch_pos = prefix_len + local_pos
    queries = rotate(exchanged[:, :, :group_heads, :], stretch_pos).astype(jnp.bfloat16)
    stretch_keys = rotate(exchanged[:, :, group_heads, :], stretch_pos).astype(jnp.bfloat16)
    stretch_values = exchanged[:, :, group_heads + 1, :]
    initial = (
        jnp.full((stretch_rows, kv_local, group_heads), -1e30, jnp.float32),
        jnp.zeros((stretch_rows, kv_local, group_heads), jnp.float32),
        jnp.zeros((stretch_rows, kv_local, group_heads, head_dim), jnp.float32),
    )
    own_pos = block_ids[0] * block_rows + jnp.arange(block_rows, dtype=jnp.int32)
    prefix_keys = rotate(decode_block(key_codes, codebooks), own_pos).astype(jnp.bfloat16)
    key_rows = lax.all_gather(prefix_keys, "outer", axis=0, tiled=True)
    value_rows = lax.all_gather(prefix_values, "outer", axis=0, tiled=True)
    length = key_rows.shape[0]
    span_rows = span_of()

    def advance(step_index, inner_state):
        first_row = step_index * span_rows
        key_part = lax.dynamic_slice_in_dim(key_rows, first_row, span_rows, 0)
        value_part = lax.dynamic_slice_in_dim(value_rows, first_row, span_rows, 0)
        return absorb(inner_state, queries, key_part, value_part, None)

    allowed = local_pos[None, :] <= local_pos[:, None]
    final_state = absorb(
        lax.fori_loop(0, length // span_rows, advance, initial),
        queries,
        stretch_keys,
        stretch_values,
        allowed,
    )
    running_max, running_sum, weighted = final_state
    outputs = (weighted / running_sum[..., None]).astype(jnp.bfloat16)
    return lax.all_to_all(outputs, "inner", split_axis=0, concat_axis=1, tiled=True)


def solution(mesh):
    return jax.shard_map(
        shards,
        mesh=mesh,
        in_specs=(
            P(("outer", "inner"), None, None, None),
            P("outer", "inner", None),
            P("inner", None, None),
            P("outer", "inner", None),
            P("outer", "inner"),
            P("outer"),
        ),
        out_specs=P(("outer", "inner"), None, None, None),
        check_vma=False,
    )
```

profile of v0, /device:TPU:32, one launch (start us, length us, event | category | flops | bytes accessed | tf_op | source)
XLA Modules:
  0.0 320.7 jit_solution(219991064677124452)
XLA Ops:
  6.6 0.8 convert_bitcast_fusion
  7.4 0.9 copy.48
  9.0 0.5 fusion.33
  9.5 0.2 fusion.61
  9.7 0.6 pad_maximum_fusion.1
  10.3 0.0 all-gather.3.cloned.1.call-update
  10.3 1.4 copy.49
  11.8 10.2 %all-to-all-start = ((bf16[64,8,10,128]{3,0,2,1:T(8,128)(2,1)}), bf16[64,8,10,128]{3,0,2,1:T(8,128)(2,1)S(1)}, u32[]{:S(2)}, u32[]{:S(2)}) async-start(bf16[64,8,10,128]{3,0,2,1:T(8,128)(2,1)} %copy.49), calls=%async_computation | async-start | bytes 2621440 | tf_op jit(solution)/shard_map/all_to_all | solution.py:73
  22.0 0.0 all-gather.5.cloned.1.call-start
  22.0 0.1 copy.51
  22.1 0.6 multiply_convert_fusion
  22.8 0.0 all-gather.5.cloned.1.call-update
  22.8 0.8 iota_compare_fusion
  23.6 1.8 multiply_cosine_fusion.1
  25.4 35.3 %all-to-all-done = bf16[64,8,10,128]{3,0,2,1:T(8,128)(2,1)S(1)} async-done(((bf16[64,8,10,128]{3,0,2,1:T(8,128)(2,1)}), bf16[64,8,10,128]{3,0,2,1:T(8,128)(2,1)S(1)}, u32[]{:S(2)}, u32[]{:S(2)}) %all-to-all-start) | async-done | bytes 1310752 | tf_op jit(solution)/shard_map/all_to_all | solution.py:73
  60.7 0.1 copy.50
  60.8 0.0 copy-start.7
  60.9 0.1 slice_convert_fusion
  61.0 1.0 copy-done.7
  62.0 0.3 copy-done.8
  62.2 0.8 subtract_convert_fusion
  63.0 0.0 copy-start.2
  63.0 0.9 copy-done
  64.0 0.6 pad_maximum_fusion
  64.6 0.7 fusion.50
  65.3 25.1 %all-gather.3.cloned.1.call-done = bf16[4096,1,128]{0,2,1:T(8,128)(2,1)} async-done(((bf16[128,1,128]{0,2,1:T(8,128)(2,1)}), bf16[4096,1,128]{0,2,1:T(8,128)(2,1)}) %all-gather.3.cloned.1.call-update) | async-done | bytes 1048592 | tf_op jit(solution)/shard_map/all_gather | solution.py:88
  90.4 67.9 %all-gather.5.cloned.1.call-done = bf16[4096,1,128]{0,2,1:T(8,128)(2,1)} async-done(((bf16[128,1,128]{0,2,1:T(8,128)(2,1)}), bf16[4096,1,128]{0,2,1:T(8,128)(2,1)}) %all-gather.5.cloned.1.call-update) | async-done | bytes 1048592 | tf_op jit(solution)/shard_map/all_gather | solution.py:89
  158.4 101.3 %while.18 = (s32[]{:T(128)}, f32[512,1,8]{0,2,1:T(8,128)S(1)}, f32[512,1,8]{0,2,1:T(8,128)S(1)}, f32[512,1,8,128]{0,3,2,1:T(8,128)S(1)}, bf16[4096,1,128]{0,2,1:...) while((s32[]{:T(128)}, f32[512,1,8]{0,2,1:T(8,128)S(1)}, ...), condition=%wide.region_3.0_spmd.clone, body=%wide.region_0.0_spmd.clone.sunk | while | flops 2182635520 | bytes 56361140 | solution.py:101
  158.4 9.1 %bitcast_reduce_fusion.2 = (f32[512,8]{0,1:T(8,128)S(1)}, f32[1024,512,8]{1,0,2:T(8,128)}) fusion(bf16[512,1,8,128]{3,0,2,1:T(8,128)(2,1)S(1)} %get-tuple-element.273, bf16[4096,1,128]{0,2,1:T(8,128)(2,1)} %get-tuple-element.272, s32[]{:T(128)S(6)} %select_n.27), kind=kOutput, calls=%fused_computation.1.clone.1 | convolution fusion | flops 1082126336 | bytes 18104324 | tf_op jit(solution)/shard_map/while/body/eval_jaxpr/tkgd,nkd->tkgn/dot_general | solution.py:47
  167.5 8.5 %fusion.77 = f32[512,8]{0,1:T(8,128)S(1)} fusion(f32[1024,512,8]{1,0,2:T(8,128)} %get-tuple-element.244, f32[512,8]{0,1:T(8,128)S(1)} %bitcast.167), kind=kLoop, calls=%fused_computation.4.clone.1 | loop fusion | flops 12578816 | bytes 16809984 | tf_op jit(solution)/shard_map/while/body/eval_jaxpr/reduce_sum | solution.py:55
  176.0 7.7 %bitcast_add_fusion.7 = f32[512,1,8,128]{0,3,2,1:T(8,128)S(1)} fusion(f32[512,1,8,128]{0,3,2,1:T(8,128)S(1)} %get-tuple-element.260, f32[1024,512,8]{1,0,2:T(8,128)} %get-tuple-element.244, f32[512,8]{0,1:T(8,128)S(1)} %bitcast.168, f32[512,8]{0,1:T(8,128)S(1)} %get-tuple-element.245, pred[]{:T(512)S(6)} %compare.3, ...), kind=kOutput, calls=%fused_computation.9.clone.1 | convolution fusion | flops 1087897600 | bytes 21266436 | tf_op jit(solution)/shard_map/while/body/eval_jaxpr/tkgn,nkd->tkgd/dot_general | solution.py:56
  183.7 9.1 %bitcast_reduce_fusion.2 = (f32[512,8]{0,1:T(8,128)S(1)}, f32[1024,512,8]{1,0,2:T(8,128)}) fusion(bf16[512,1,8,128]{3,0,2,1:T(8,128)(2,1)S(1)} %get-tuple-element.273, bf16[4096,1,128]{0,2,1:T(8,128)(2,1)} %get-tuple-element.272, s32[]{:T(128)S(6)} %select_n.27), kind=kOutput, calls=%fused_computation.1.clone.1 | convolution fusion | flops 1082126336 | bytes 18104324 | tf_op jit(solution)/shard_map/while/body/eval_jaxpr/tkgd,nkd->tkgn/dot_general | solution.py:47
  192.8 8.5 %fusion.77 = f32[512,8]{0,1:T(8,128)S(1)} fusion(f32[1024,512,8]{1,0,2:T(8,128)} %get-tuple-element.244, f32[512,8]{0,1:T(8,128)S(1)} %bitcast.167), kind=kLoop, calls=%fused_computation.4.clone.1 | loop fusion | flops 12578816 | bytes 16809984 | tf_op jit(solution)/shard_map/while/body/eval_jaxpr/reduce_sum | solution.py:55
  201.3 7.7 %bitcast_add_fusion.7 = f32[512,1,8,128]{0,3,2,1:T(8,128)S(1)} fusion(f32[512,1,8,128]{0,3,2,1:T(8,128)S(1)} %get-tuple-element.260, f32[1024,512,8]{1,0,2:T(8,128)} %get-tuple-element.244, f32[512,8]{0,1:T(8,128)S(1)} %bitcast.168, f32[512,8]{0,1:T(8,128)S(1)} %get-tuple-element.245, pred[]{:T(512)S(6)} %compare.3, ...), kind=kOutput, calls=%fused_computation.9.clone.1 | convolution fusion | flops 1087897600 | bytes 21266436 | tf_op jit(solution)/shard_map/while/body/eval_jaxpr/tkgn,nkd->tkgd/dot_general | solution.py:56
  209.0 9.1 %bitcast_reduce_fusion.2 = (f32[512,8]{0,1:T(8,128)S(1)}, f32[1024,512,8]{1,0,2:T(8,128)}) fusion(bf16[512,1,8,128]{3,0,2,1:T(8,128)(2,1)S(1)} %get-tuple-element.273, bf16[4096,1,128]{0,2,1:T(8,128)(2,1)} %get-tuple-element.272, s32[]{:T(128)S(6)} %select_n.27), kind=kOutput, calls=%fused_computation.1.clone.1 | convolution fusion | flops 1082126336 | bytes 18104324 | tf_op jit(solution)/shard_map/while/body/eval_jaxpr/tkgd,nkd->tkgn/dot_general | solution.py:47
  218.1 8.5 %fusion.77 = f32[512,8]{0,1:T(8,128)S(1)} fusion(f32[1024,512,8]{1,0,2:T(8,128)} %get-tuple-element.244, f32[512,8]{0,1:T(8,128)S(1)} %bitcast.167), kind=kLoop, calls=%fused_computation.4.clone.1 | loop fusion | flops 12578816 | bytes 16809984 | tf_op jit(solution)/shard_map/while/body/eval_jaxpr/reduce_sum | solution.py:55
  226.7 7.7 %bitcast_add_fusion.7 = f32[512,1,8,128]{0,3,2,1:T(8,128)S(1)} fusion(f32[512,1,8,128]{0,3,2,1:T(8,128)S(1)} %get-tuple-element.260, f32[1024,512,8]{1,0,2:T(8,128)} %get-tuple-element.244, f32[512,8]{0,1:T(8,128)S(1)} %bitcast.168, f32[512,8]{0,1:T(8,128)S(1)} %get-tuple-element.245, pred[]{:T(512)S(6)} %compare.3, ...), kind=kOutput, calls=%fused_computation.9.clone.1 | convolution fusion | flops 1087897600 | bytes 21266436 | tf_op jit(solution)/shard_map/while/body/eval_jaxpr/tkgn,nkd->tkgd/dot_general | solution.py:56
  234.4 9.1 %bitcast_reduce_fusion.2 = (f32[512,8]{0,1:T(8,128)S(1)}, f32[1024,512,8]{1,0,2:T(8,128)}) fusion(bf16[512,1,8,128]{3,0,2,1:T(8,128)(2,1)S(1)} %get-tuple-element.273, bf16[4096,1,128]{0,2,1:T(8,128)(2,1)} %get-tuple-element.272, s32[]{:T(128)S(6)} %select_n.27), kind=kOutput, calls=%fused_computation.1.clone.1 | convolution fusion | flops 1082126336 | bytes 18104324 | tf_op jit(solution)/shard_map/while/body/eval_jaxpr/tkgd,nkd->tkgn/dot_general | solution.py:47
  243.5 8.5 %fusion.77 = f32[512,8]{0,1:T(8,128)S(1)} fusion(f32[1024,512,8]{1,0,2:T(8,128)} %get-tuple-element.244, f32[512,8]{0,1:T(8,128)S(1)} %bitcast.167), kind=kLoop, calls=%fused_computation.4.clone.1 | loop fusion | flops 12578816 | bytes 16809984 | tf_op jit(solution)/shard_map/while/body/eval_jaxpr/reduce_sum | solution.py:55
  252.0 7.7 %bitcast_add_fusion.7 = f32[512,1,8,128]{0,3,2,1:T(8,128)S(1)} fusion(f32[512,1,8,128]{0,3,2,1:T(8,128)S(1)} %get-tuple-element.260, f32[1024,512,8]{1,0,2:T(8,128)} %get-tuple-element.244, f32[512,8]{0,1:T(8,128)S(1)} %bitcast.168, f32[512,8]{0,1:T(8,128)S(1)} %get-tuple-element.245, pred[]{:T(512)S(6)} %compare.3, ...), kind=kOutput, calls=%fused_computation.9.clone.1 | convolution fusion | flops 1087897600 | bytes 21266436 | tf_op jit(solution)/shard_map/while/body/eval_jaxpr/tkgn,nkd->tkgd/dot_general | solution.py:56
  259.7 1.8 copy.53
  261.5 2.4 fusion.54
  263.9 3.4 %fusion.22 = (f32[512,8]{0,1:T(8,128)S(1)}, f32[512,512,8]{1,0,2:T(8,128)S(1)}) fusion(pred[512,512]{0,1:T(8,128)(4,1)S(1)} %copy-done.4, bf16[512,8,64]{2,0,1:T(8,128)(2,1)} %bitcast.170, bf16[512,8,64]{2,0,1:T(8,128)(2,1)S(1)} %bitcast.169, bf16[512,64]{1,0:T(8,128)(2,1)S(1)} %get-tuple-element.186, bf16[512,64]{1,0:T(8,128)(2,1)S(1)} %get-tuple-element.185), kind=kOutput, calls=%fused_computation.29 | convolution fusion | flops 545517568 | bytes 9846784 | tf_op jit(solution)/shard_map/tkgd,nkd->tkgn/dot_general | solution.py:47
  267.4 1.7 fusion.20
  269.2 4.1 %fusion.28 = bf16[512,1,8,128]{3,0,2,1:T(8,128)(2,1)S(1)} fusion(f32[512,1,8,128]{3,0,2,1:T(8,128)S(1)} %copy-done.5, f32[512,512,8]{1,0,2:T(8,128)S(1)} %get-tuple-element.194, f32[512,8]{0,1:T(8,128)S(1)} %fusion.65, pred[512,512]{0,1:T(8,128)(4,1)S(1)} %copy-done.4, f32[512,8]{0,1:T(8,128)S(1)} %get-tuple-element.190, ...), kind=kOutput, calls=%fused_computation.35 | convolution fusion | flops 547356672 | bytes 11976704 | tf_op jit(solution)/shard_map/tkgn,nkd->tkgd/dot_general | solution.py:56
  273.3 0.7 copy.55
  274.0 38.6 %all_to_all.36 = bf16[512,1,8,128]{3,2,1,0:T(8,128)(2,1)S(1)} all-to-all(bf16[512,1,8,128]{3,2,1,0:T(8,128)(2,1)S(1)} %copy.55), channel_id=1, replica_groups=mesh['outer'=32,'inner'=8] {'inner'}, dimensions={0} | all-to-all | bytes 2097152 | tf_op jit(solution)/shard_map/all_to_all | solution.py:109
  312.6 1.3 copy.61
  (39 shorter events, 0.2 us)
Async XLA Ops:
  6.5 3.8 %copy-start.6 = (bf16[64,8,10,128]{3,1,2,0:T(8,128)(2,1)S(1)}, bf16[64,8,10,128]{3,1,2,0:T(8,128)(2,1)}, u32[]{:S(2)}) copy-start(bf16[64,8,10,128]{3,1,2,0:T(8,128)(2,1)} %param.8) | copy-start | bytes 3932164
  6.5 83.9 %all-gather.3.cloned.1.call-start = ((), (), s32[]{:S(2)}) async-start(), calls=%async_computation.2 | async-start | bytes 1081344 | tf_op jit(solution)/shard_map/all_gather | solution.py:88
  10.3 11.7 %copy-start.9 = (bf16[128,1,128]{2,0,1:T(8,128)(2,1)S(1)}, bf16[128,1,128]{2,0,1:T(8,128)(2,1)}, u32[]{:S(2)}) copy-start(bf16[128,1,128]{2,0,1:T(8,128)(2,1)} %param.11) | copy-start | bytes 98308
  10.3 11.8 %copy-start.10 = (f32[128,1]{0,1:T(1,128)S(1)}, f32[128,1]{0,1:T(1,128)}, u32[]{:S(2)}) copy-start(f32[128,1]{0,1:T(1,128)} %param.12) | copy-start | bytes 1540
  11.8 48.9 %all-to-all-start = ((bf16[64,8,10,128]{3,0,2,1:T(8,128)(2,1)}), bf16[64,8,10,128]{3,0,2,1:T(8,128)(2,1)S(1)}, u32[]{:S(2)}, u32[]{:S(2)}) async-start(bf16[64,8,10,128]{3,0,2,1:T(8,128)(2,1)} %copy.49), calls=%async_computation | async-start | bytes 2621440 | tf_op jit(solution)/shard_map/all_to_all | solution.py:73
  22.0 136.4 %all-gather.5.cloned.1.call-start = ((), (), s32[]{:S(2)}) async-start(), calls=%async_computation.3 | async-start | bytes 1081344 | tf_op jit(solution)/shard_map/all_gather | solution.py:89
  60.8 3.7 %copy-start.3 = (bf16[8,64,1,10,128]{4,1,0,3,2:T(8,128)(2,1)}, bf16[8,64,1,10,128]{4,1,0,3,2:T(8,128)(2,1)S(1)}, u32[]{:S(2)}) copy-start(bf16[8,64,1,10,128]{4,1,0,3,2:T(8,128)(2,1)S(1)} %copy.50) | copy-start | bytes 3932164
  60.8 1.1 copy-start.7
  60.8 1.4 copy-start.8
  63.0 1.0 copy-start
  63.0 1.6 copy-start.2
  259.7 4.2 %copy-start.1 = (bf16[512,1,8,64]{3,0,2,1:T(8,128)(2,1)S(1)}, bf16[512,1,8,64]{3,0,2,1:T(8,128)(2,1)}, u32[]{:S(2)}) copy-start(bf16[512,1,8,64]{3,0,2,1:T(8,128)(2,1)} %copy-done) | copy-start | bytes 1572868
  259.7 4.2 %copy-start.4 = (pred[512,512]{0,1:T(8,128)(4,1)S(1)}, pred[512,512]{0,1:T(8,128)(4,1)}, u32[]{:S(2)}) copy-start(pred[512,512]{0,1:T(8,128)(4,1)} %iota_compare_fusion) | copy-start | bytes 786436
  267.4 1.8 copy-start.5
Sparse Core Ops, SparseCore 0:
  10.4 79.9 all-gather.2
  92.2 66.1 all-gather.4
where the time goes:
time: 321 us
  waiting for transfers between devices  128 us (40%)
  matrix products  75.1 us (23%)
  other arithmetic  45.3 us (14%)
  blocking collectives  38.6 us (12%)
  between operations  14.3 us (4%)
  starting transfers between devices  10.2 us (3%)
  local copies, waits for them, and re-layouts  8.6 us (3%)
    all_gather x1, waiting for transfers between devices, shards(): value_rows = lax.all_gather(prefix_values, 'outer', axis=0, tiled=True)  67.9 us
    dot_general x5, matrix products, absorb(): jnp.einsum('tkgd,nkd->tkgn', queries, key_rows, preferred_element_type=jn...  39.8 us
    all_to_all x1, blocking collectives, shards(): lax.all_to_all(outputs, 'inner', split_axis=0, concat_axis=1, tiled=True)  38.6 us
    reduce_sum x5, other arithmetic, absorb(): running_sum = running_sum * decay_factor + jnp.sum(weights, axis=-1)  35.7 us
    all_to_all x1, waiting for transfers between devices, shards(): lax.all_to_all(qkv, 'inner', split_axis=1, concat_axis=0, tiled=True)  35.3 us
    dot_general x5, matrix products, absorb(): jnp.einsum('tkgn,nkd->tkgd', weights.astype(jnp.bfloat16), value_rows, pr...  34.8 us
    all_gather x1, waiting for transfers between devices, shards(): key_rows = lax.all_gather(prefix_keys, 'outer', axis=0, tiled=True)  25.1 us
    all_to_all x1, starting transfers between devices, shards(): lax.all_to_all(qkv, 'inner', split_axis=1, concat_axis=0, tiled=True)  10.2 us
  transfers between devices with their start and end apart: 3, of which 3 were waited for; matrix products, arithmetic and copies ran while one was open for 2% of the time, Pallas kernels for 0%

commit v1 on v0

--- a/solution.py
+++ b/solution.py
@@ -70,7 +70,10 @@
     prefix_values = (value_codes.astype(jnp.float32) * value_scales[:, :, None]).astype(
         jnp.bfloat16
     )
-    exchanged = lax.all_to_all(qkv, "inner", split_axis=1, concat_axis=0, tiled=True)
+    exchanged = jnp.concatenate(
+        lax.all_to_all(jnp.stack(jnp.split(qkv, lax.axis_size("inner"), axis=1)), "inner", 0, 0),
+        axis=0,
+    )
     stretch_rows = exchanged.shape[0]
     kv_local = exchanged.shape[1]
     local_pos = jnp.arange(stretch_rows, dtype=jnp.int32)

time: 321 us -> 320 us (level)
  waiting for transfers between devices: 128 us -> 122 us
  local copies, waits for them, and re-layouts: 8.6 us -> 13.2 us
    all_gather x1, waiting for transfers between devices: 25.1 us -> 18.5 us  [shards(): key_rows = lax.all_gather(prefix_keys, 'outer', axis=0, tiled=True)]
    unnamed x25 -> x27, local copies, waits for them, and re-layouts: 4.7 us -> 8.12 us
  transfers between devices with their start and end apart: 3 -> 3, of which waited for: 3 -> 3; matrix products, arithmetic and copies ran while one was open for 2% -> 4% of each run, Pallas kernels for 0% -> 0%
where the time goes in v1:
time: 320 us; the launch traced here: 319 us
  waiting for transfers between devices  122 us (38%)
  matrix products  74.6 us (23%)
  other arithmetic  45.3 us (14%)
  blocking collectives  38.6 us (12%)
  between operations  14.3 us (4%)
  local copies, waits for them, and re-layouts  13.2 us (4%)
  starting transfers between devices  10.4 us (3%)
    all_gather x1, waiting for transfers between devices, shards(): value_rows = lax.all_gather(prefix_values, 'outer', axis=0, tiled=True)  68.7 us
    dot_general x5, matrix products, absorb(): jnp.einsum('tkgd,nkd->tkgn', queries, key_rows, preferred_element_type=jn...  40.1 us
    all_to_all x1, blocking collectives, shards(): lax.all_to_all(outputs, 'inner', split_axis=0, concat_axis=1, tiled=True)  38.6 us
    reduce_sum x5, other arithmetic, absorb(): running_sum = running_sum * decay_factor + jnp.sum(weights, axis=-1)  35.7 us
    all_to_all x1, waiting for transfers between devices, shards(): lax.all_to_all(jnp.stack(jnp.split(qkv, lax.axis_size('inner'), axis=1)),...  35.1 us
    dot_general x5, matrix products, absorb(): jnp.einsum('tkgn,nkd->tkgd', weights.astype(jnp.bfloat16), value_rows, pr...  34 us
    all_gather x1, waiting for transfers between devices, shards(): key_rows = lax.all_gather(prefix_keys, 'outer', axis=0, tiled=True)  18.5 us
    all_to_all x1, starting transfers between devices, shards(): lax.all_to_all(jnp.stack(jnp.split(qkv, lax.axis_size('inner'), axis=1)),...  10.2 us
  transfers between devices with their start and end apart: 3, of which 3 were waited for; matrix products, arithmetic and copies ran while one was open for 4% of the time, Pallas kernels for 0%

profile of v1, /device:TPU:32, one launch (start us, length us, event | category | flops | bytes accessed | tf_op | source)
XLA Modules:
  0.0 319.0 jit_solution(16170967276454808180)
XLA Ops:
  6.6 0.8 convert_bitcast_fusion
  7.4 0.9 copy.60
  9.0 0.5 fusion.33
  9.5 0.2 fusion.69
  9.7 0.6 pad_maximum_fusion.1
  10.3 2.2 fusion.78
  12.5 0.7 fusion.57
  13.2 0.7 fusion.56
  13.9 0.7 fusion.55
  14.6 0.7 fusion.54
  15.3 0.7 fusion.53
  16.0 0.7 fusion.52
  16.7 0.7 fusion.51
  17.4 0.7 fusion.50
  18.1 10.2 %all-to-all-start = ((bf16[8,64,1,10,128]{4,1,3,2,0:T(8,128)(2,1)}), bf16[8,64,1,10,128]{4,1,3,2,0:T(8,128)(2,1)S(1)}, u32[]{:S(2)}, u32[]{:S(2)}) async-start(bf16[8,64,1,10,128]{4,1,3,2,0:T(8,128)(2,1)} %fusion.50), calls=%async_computation | async-start | bytes 2621440 | tf_op jit(solution)/shard_map/all_to_all | solution.py:74
  28.3 0.2 all-gather.5.cloned.1.call-start
  28.7 0.6 multiply_convert_fusion
  29.3 0.8 iota_compare_fusion
  30.1 1.8 multiply_cosine_fusion.1
  31.9 35.1 %all-to-all-done = bf16[8,64,1,10,128]{4,1,3,2,0:T(8,128)(2,1)S(1)} async-done(((bf16[8,64,1,10,128]{4,1,3,2,0:T(8,128)(2,1)}), bf16[8,64,1,10,128]{4,1,3,2,0:T(8,128)(2,1)S(1)}, u32[]{:S(2)}, u32[]{:S(2)}) %all-to-all-start) | async-done | bytes 1310752 | tf_op jit(solution)/shard_map/all_to_all | solution.py:74
  67.3 1.0 copy-done.5
  68.3 0.3 copy-done.6
  68.6 0.8 subtract_convert_fusion
  69.4 0.9 copy-done
  70.3 0.6 pad_maximum_fusion
  70.9 0.7 fusion.58
  71.7 18.5 %all-gather.3.cloned.1.call-done = bf16[4096,1,128]{0,2,1:T(8,128)(2,1)} async-done(((bf16[128,1,128]{0,2,1:T(8,128)(2,1)}), bf16[4096,1,128]{0,2,1:T(8,128)(2,1)}) %all-gather.3.cloned.1.call-update) | async-done | bytes 1048592 | tf_op jit(solution)/shard_map/all_gather | solution.py:91
  90.2 68.7 %all-gather.5.cloned.1.call-done = bf16[4096,1,128]{0,2,1:T(8,128)(2,1)} async-done(((bf16[128,1,128]{0,2,1:T(8,128)(2,1)}), bf16[4096,1,128]{0,2,1:T(8,128)(2,1)}) %all-gather.5.cloned.1.call-update) | async-done | bytes 1048592 | tf_op jit(solution)/shard_map/all_gather | solution.py:92
  158.9 101.3 %while.18 = (s32[]{:T(128)}, f32[512,1,8]{0,2,1:T(8,128)S(1)}, f32[512,1,8]{0,2,1:T(8,128)S(1)}, f32[512,1,8,128]{0,3,2,1:T(8,128)S(1)}, bf16[4096,1,128]{0,2,1:...) while((s32[]{:T(128)}, f32[512,1,8]{0,2,1:T(8,128)S(1)}, ...), condition=%wide.region_3.0_spmd.clone, body=%wide.region_0.0_spmd.clone.sunk | while | flops 2182635520 | bytes 56361140 | solution.py:104
  158.9 9.1 %bitcast_reduce_fusion.2 = (f32[512,8]{0,1:T(8,128)S(1)}, f32[1024,512,8]{1,0,2:T(8,128)}) fusion(bf16[512,1,8,128]{3,0,2,1:T(8,128)(2,1)S(1)} %get-tuple-element.281, bf16[4096,1,128]{0,2,1:T(8,128)(2,1)} %get-tuple-element.280, s32[]{:T(128)S(6)} %select_n.27), kind=kOutput, calls=%fused_computation.1.clone.1 | convolution fusion | flops 1082126336 | bytes 18104324 | tf_op jit(solution)/shard_map/while/body/eval_jaxpr/tkgd,nkd->tkgn/dot_general | solution.py:47
  168.0 8.5 %fusion.86 = f32[512,8]{0,1:T(8,128)S(1)} fusion(f32[1024,512,8]{1,0,2:T(8,128)} %get-tuple-element.252, f32[512,8]{0,1:T(8,128)S(1)} %bitcast.193), kind=kLoop, calls=%fused_computation.4.clone.1 | loop fusion | flops 12578816 | bytes 16809984 | tf_op jit(solution)/shard_map/while/body/eval_jaxpr/reduce_sum | solution.py:55
  176.6 7.7 %bitcast_add_fusion.7 = f32[512,1,8,128]{0,3,2,1:T(8,128)S(1)} fusion(f32[512,1,8,128]{0,3,2,1:T(8,128)S(1)} %get-tuple-element.268, f32[1024,512,8]{1,0,2:T(8,128)} %get-tuple-element.252, f32[512,8]{0,1:T(8,128)S(1)} %bitcast.194, f32[512,8]{0,1:T(8,128)S(1)} %get-tuple-element.253, pred[]{:T(512)S(6)} %compare.3, ...), kind=kOutput, calls=%fused_computation.9.clone.1 | convolution fusion | flops 1087897600 | bytes 21266436 | tf_op jit(solution)/shard_map/while/body/eval_jaxpr/tkgn,nkd->tkgd/dot_general | solution.py:56
  184.3 9.1 %bitcast_reduce_fusion.2 = (f32[512,8]{0,1:T(8,128)S(1)}, f32[1024,512,8]{1,0,2:T(8,128)}) fusion(bf16[512,1,8,128]{3,0,2,1:T(8,128)(2,1)S(1)} %get-tuple-element.281, bf16[4096,1,128]{0,2,1:T(8,128)(2,1)} %get-tuple-element.280, s32[]{:T(128)S(6)} %select_n.27), kind=kOutput, calls=%fused_computation.1.clone.1 | convolution fusion | flops 1082126336 | bytes 18104324 | tf_op jit(solution)/shard_map/while/body/eval_jaxpr/tkgd,nkd->tkgn/dot_general | solution.py:47
  193.4 8.5 %fusion.86 = f32[512,8]{0,1:T(8,128)S(1)} fusion(f32[1024,512,8]{1,0,2:T(8,128)} %get-tuple-element.252, f32[512,8]{0,1:T(8,128)S(1)} %bitcast.193), kind=kLoop, calls=%fused_computation.4.clone.1 | loop fusion | flops 12578816 | bytes 16809984 | tf_op jit(solution)/shard_map/while/body/eval_jaxpr/reduce_sum | solution.py:55
  201.9 7.7 %bitcast_add_fusion.7 = f32[512,1,8,128]{0,3,2,1:T(8,128)S(1)} fusion(f32[512,1,8,128]{0,3,2,1:T(8,128)S(1)} %get-tuple-element.268, f32[1024,512,8]{1,0,2:T(8,128)} %get-tuple-element.252, f32[512,8]{0,1:T(8,128)S(1)} %bitcast.194, f32[512,8]{0,1:T(8,128)S(1)} %get-tuple-element.253, pred[]{:T(512)S(6)} %compare.3, ...), kind=kOutput, calls=%fused_computation.9.clone.1 | convolution fusion | flops 1087897600 | bytes 21266436 | tf_op jit(solution)/shard_map/while/body/eval_jaxpr/tkgn,nkd->tkgd/dot_general | solution.py:56
  209.6 9.1 %bitcast_reduce_fusion.2 = (f32[512,8]{0,1:T(8,128)S(1)}, f32[1024,512,8]{1,0,2:T(8,128)}) fusion(bf16[512,1,8,128]{3,0,2,1:T(8,128)(2,1)S(1)} %get-tuple-element.281, bf16[4096,1,128]{0,2,1:T(8,128)(2,1)} %get-tuple-element.280, s32[]{:T(128)S(6)} %select_n.27), kind=kOutput, calls=%fused_computation.1.clone.1 | convolution fusion | flops 1082126336 | bytes 18104324 | tf_op jit(solution)/shard_map/while/body/eval_jaxpr/tkgd,nkd->tkgn/dot_general | solution.py:47
  218.7 8.5 %fusion.86 = f32[512,8]{0,1:T(8,128)S(1)} fusion(f32[1024,512,8]{1,0,2:T(8,128)} %get-tuple-element.252, f32[512,8]{0,1:T(8,128)S(1)} %bitcast.193), kind=kLoop, calls=%fused_computation.4.clone.1 | loop fusion | flops 12578816 | bytes 16809984 | tf_op jit(solution)/shard_map/while/body/eval_jaxpr/reduce_sum | solution.py:55
  227.2 7.7 %bitcast_add_fusion.7 = f32[512,1,8,128]{0,3,2,1:T(8,128)S(1)} fusion(f32[512,1,8,128]{0,3,2,1:T(8,128)S(1)} %get-tuple-element.268, f32[1024,512,8]{1,0,2:T(8,128)} %get-tuple-element.252, f32[512,8]{0,1:T(8,128)S(1)} %bitcast.194, f32[512,8]{0,1:T(8,128)S(1)} %get-tuple-element.253, pred[]{:T(512)S(6)} %compare.3, ...), kind=kOutput, calls=%fused_computation.9.clone.1 | convolution fusion | flops 1087897600 | bytes 21266436 | tf_op jit(solution)/shard_map/while/body/eval_jaxpr/tkgn,nkd->tkgd/dot_general | solution.py:56
  234.9 9.1 %bitcast_reduce_fusion.2 = (f32[512,8]{0,1:T(8,128)S(1)}, f32[1024,512,8]{1,0,2:T(8,128)}) fusion(bf16[512,1,8,128]{3,0,2,1:T(8,128)(2,1)S(1)} %get-tuple-element.281, bf16[4096,1,128]{0,2,1:T(8,128)(2,1)} %get-tuple-element.280, s32[]{:T(128)S(6)} %select_n.27), kind=kOutput, calls=%fused_computation.1.clone.1 | convolution fusion | flops 1082126336 | bytes 18104324 | tf_op jit(solution)/shard_map/while/body/eval_jaxpr/tkgd,nkd->tkgn/dot_general | solution.py:47
  244.0 8.5 %fusion.86 = f32[512,8]{0,1:T(8,128)S(1)} fusion(f32[1024,512,8]{1,0,2:T(8,128)} %get-tuple-element.252, f32[512,8]{0,1:T(8,128)S(1)} %bitcast.193), kind=kLoop, calls=%fused_computation.4.clone.1 | loop fusion | flops 12578816 | bytes 16809984 | tf_op jit(solution)/shard_map/while/body/eval_jaxpr/reduce_sum | solution.py:55
  252.6 7.7 %bitcast_add_fusion.7 = f32[512,1,8,128]{0,3,2,1:T(8,128)S(1)} fusion(f32[512,1,8,128]{0,3,2,1:T(8,128)S(1)} %get-tuple-element.268, f32[1024,512,8]{1,0,2:T(8,128)} %get-tuple-element.252, f32[512,8]{0,1:T(8,128)S(1)} %bitcast.194, f32[512,8]{0,1:T(8,128)S(1)} %get-tuple-element.253, pred[]{:T(512)S(6)} %compare.3, ...), kind=kOutput, calls=%fused_computation.9.clone.1 | convolution fusion | flops 1087897600 | bytes 21266436 | tf_op jit(solution)/shard_map/while/body/eval_jaxpr/tkgn,nkd->tkgd/dot_general | solution.py:56
  260.2 2.4 fusion.62
  262.7 3.7 %fusion.22 = (f32[512,8]{0,1:T(8,128)S(1)}, f32[512,512,8]{1,0,2:T(8,128)S(1)}) fusion(pred[512,512]{0,1:T(8,128)(4,1)S(1)} %copy-done.4, bf16[512,8,64]{2,0,1:T(8,128)(2,1)} %bitcast.196, bf16[512,8,64]{2,0,1:T(8,128)(2,1)} %bitcast.195, bf16[512,64]{1,0:T(8,128)(2,1)S(1)} %get-tuple-element.194, bf16[512,64]{1,0:T(8,128)(2,1)S(1)} %get-tuple-element.193), kind=kOutput, calls=%fused_computation.29 | convolution fusion | flops 545517568 | bytes 9846784 | tf_op jit(solution)/shard_map/tkgd,nkd->tkgn/dot_general | solution.py:47
  266.4 1.7 fusion.20
  268.2 3.3 %fusion.28 = bf16[512,1,8,128]{0,3,2,1:T(8,128)(2,1)S(1)} fusion(f32[512,1,8,128]{0,3,2,1:T(8,128)S(1)} %get-tuple-element.131, f32[512,512,8]{1,0,2:T(8,128)S(1)} %get-tuple-element.202, f32[512,8]{0,1:T(8,128)S(1)} %fusion.73, pred[512,512]{0,1:T(8,128)(4,1)S(1)} %copy-done.4, f32[512,8]{0,1:T(8,128)S(1)} %get-tuple-element.198, ...), kind=kOutput, calls=%fused_computation.35 | convolution fusion | flops 547356672 | bytes 11976704 | tf_op jit(solution)/shard_map/tkgn,nkd->tkgd/dot_general | solution.py:56
  271.5 0.8 copy.74
  272.3 38.6 %all_to_all.23 = bf16[512,1,8,128]{3,2,1,0:T(8,128)(2,1)S(1)} all-to-all(bf16[512,1,8,128]{3,2,1,0:T(8,128)(2,1)S(1)} %copy.74), channel_id=1, replica_groups=mesh['outer'=32,'inner'=8] {'inner'}, dimensions={0} | all-to-all | bytes 2097152 | tf_op jit(solution)/shard_map/all_to_all | solution.py:112
  310.9 1.3 copy.75
  (42 shorter events, 0.6 us)
Async XLA Ops:
  6.5 3.8 %copy-start.2 = (bf16[64,8,10,128]{3,1,2,0:T(8,128)(2,1)S(1)}, bf16[64,8,10,128]{3,1,2,0:T(8,128)(2,1)}, u32[]{:S(2)}) copy-start(bf16[64,8,10,128]{3,1,2,0:T(8,128)(2,1)} %param.8) | copy-start | bytes 3932164
  6.5 83.6 %all-gather.3.cloned.1.call-start = ((), (), s32[]{:S(2)}) async-start(), calls=%async_computation.2 | async-start | bytes 1081344 | tf_op jit(solution)/shard_map/all_gather | solution.py:91
  16.0 12.5 %copy-start.7 = (bf16[128,1,128]{2,0,1:T(8,128)(2,1)S(1)}, bf16[128,1,128]{2,0,1:T(8,128)(2,1)}, u32[]{:S(2)}) copy-start(bf16[128,1,128]{2,0,1:T(8,128)(2,1)} %param.11) | copy-start | bytes 98308
  16.0 12.6 %copy-start.8 = (f32[128,1]{0,1:T(1,128)S(1)}, f32[128,1]{0,1:T(1,128)}, u32[]{:S(2)}) copy-start(f32[128,1]{0,1:T(1,128)} %param.12) | copy-start | bytes 1540
  18.1 48.9 %all-to-all-start = ((bf16[8,64,1,10,128]{4,1,3,2,0:T(8,128)(2,1)}), bf16[8,64,1,10,128]{4,1,3,2,0:T(8,128)(2,1)S(1)}, u32[]{:S(2)}, u32[]{:S(2)}) async-start(bf16[8,64,1,10,128]{4,1,3,2,0:T(8,128)(2,1)} %fusion.50), calls=%async_computation | async-start | bytes 2621440 | tf_op jit(solution)/shard_map/all_to_all | solution.py:74
  28.3 130.6 %all-gather.5.cloned.1.call-start = ((), (), s32[]{:S(2)}) async-start(), calls=%async_computation.3 | async-start | bytes 1081344 | tf_op jit(solution)/shard_map/all_gather | solution.py:92
  67.2 3.7 %copy-start.3 = (bf16[8,64,1,10,128]{4,1,0,3,2:T(8,128)(2,1)}, bf16[8,64,1,10,128]{4,1,0,3,2:T(8,128)(2,1)S(1)}, u32[]{:S(2)}) copy-start(bf16[8,64,1,10,128]{4,1,0,3,2:T(8,128)(2,1)S(1)} %copy.69) | copy-start | bytes 3932164
  67.2 1.1 copy-start.5
  67.2 1.4 copy-start.6
  69.4 1.0 copy-start
  69.4 1.5 copy-start.1
  158.9 103.8 %copy-start.4 = (pred[512,512]{0,1:T(8,128)(4,1)S(1)}, pred[512,512]{0,1:T(8,128)(4,1)}, u32[]{:S(2)}) copy-start(pred[512,512]{0,1:T(8,128)(4,1)} %iota_compare_fusion) | copy-start | bytes 786436
Sparse Core Ops, SparseCore 0:
  10.4 79.6 all-gather.2
  91.9 66.9 all-gather.4
